TPU v7x, 32 devices: a whole 2x2x4 slice. The times are simulated.
32 devices in a mesh: pair: 8 (over z, y), occ: 4 (over x, core).
Axes of the slice: x: 2, y: 2, z: 4, core: 2. Of those that a mesh axis runs over, the one named last changes fastest.
Arguments:
- half_ints: bfloat16 [2, 896, 4, 896], P(None, 'pair', 'occ'), may hold values from -6 to 6
- coeffs: bfloat16 [896, 768], P('occ'), may hold values from -0.1875 to 0.1875
- pair_map: int32 [8], replicated, may hold values from 0 to 7, each once
- tile_table: int32 [8], replicated, may hold values from 0 to 7, each once
Outputs:
- mo_ints: float32 [1536, 4, 768], P('pair', 'occ')
Inputs may be any that keep to these rules, and one draw needn't show every extreme that they name: pair_map is a permutation of 0 to 7. tile_table is a permutation of 0 to 7.
All inputs are finite; a program needn't handle non-finite values.
Results may differ from a plain program's by a relative error of at most 0.0029.
Values may be sent and summed in bfloat16 or wider, within the bound.
A program may use at most 64 MiB of HBM per device.

v0:
```python
import jax
import jax.numpy as jnp
from jax import lax
from jax.sharding import PartitionSpec as P


def shards(half_ints, coeffs, pair_map, tile_table):
    num_occ = half_ints.shape[0]
    sblock = half_ints.shape[1]
    local_j = half_ints.shape[2]
    num_basis = half_ints.shape[3]
    num_virt = coeffs.shape[1]
    num_pair = lax.axis_size("pair")
    tile_rows = num_occ * num_virt // num_pair
    all_coeffs = lax.all_gather(coeffs, "occ", axis=0, tiled=True)
    flat_ints = half_ints.reshape(num_occ * sblock * local_j, num_basis)
    half_mo = jnp.dot(flat_ints, all_coeffs, preferred_element_type=jnp.float32).astype(
        jnp.bfloat16
    )
    half_mo = half_mo.reshape(num_occ, sblock, local_j, num_virt)
    tile_id = tile_table[lax.axis_index("pair")]
    virt_start = tile_id * tile_rows % num_virt
    column_coeffs = lax.dynamic_slice_in_dim(all_coeffs, virt_start, tile_rows, 1)
    half_flat = half_mo.reshape(num_occ, sblock, local_j * num_virt)
    slot_occ = tile_table * tile_rows // num_virt
    outgoing = jnp.take(half_flat, slot_occ, axis=0)
    incoming = lax.all_to_all(outgoing, "pair", split_axis=0, concat_axis=0, tiled=True)
    block_coeffs = jnp.take(column_coeffs.reshape(num_pair, sblock, tile_rows), pair_map, axis=0)
    result = jnp.einsum("psa,psc->ac", block_coeffs, incoming, preferred_element_type=jnp.float32)
    return result.reshape(tile_rows, local_j, num_virt)


def solution(mesh):
    placed = (P(None, "pair", "occ", None), P("occ", None), P(), P())
    return jax.shard_map(
        shards, mesh=mesh, in_specs=placed, out_specs=P("pair", "occ", None), check_vma=False
    )
```

profile of v0, /device:TPU:0, one launch (start us, length us, event | category | flops | bytes accessed | tf_op | source)
XLA Modules:
  0.0 81.7 jit_solution(1994332243182711382)
XLA Ops:
  6.5 0.0 copy-start
  6.5 0.0 all-gather.2.cloned.1.call-start
  6.5 0.7 all-gather.2.cloned.1.call-update
  7.3 0.7 compare_and_fusion
  7.9 22.2 %all-gather.2.cloned.1.call-done = bf16[896,768]{1,0:T(8,128)(2,1)} async-done(((bf16[224,768]{1,0:T(8,128)(2,1)}), bf16[896,768]{1,0:T(8,128)(2,1)}) %all-gather.2.cloned.1.call-update) | async-done | bytes 1376272 | tf_op jit(solution)/shard_map/all_gather | solution.py:15
  30.2 0.0 copy-done
  30.2 1.9 %convolution_convert_fusion = bf16[224,768]{1,0:T(8,128)(2,1)S(1)} fusion(bf16[224,896]{1,0:T(8,128)(2,1)S(1)} %bitcast.10, bf16[896,768]{1,0:T(8,128)(2,1)} %all-gather.2.cloned.1.call-done), kind=kOutput, calls=%fused_computation.4 | convolution fusion | flops 308453376 | bytes 2121728 | tf_op jit(solution)/shard_map/dot_general | solution.py:17
  32.1 0.6 gather_fusion.1
  32.7 1.3 %broadcast_select_fusion = bf16[8,112,768]{2,1,0:T(8,128)(2,1)} fusion(bf16[8,112,768]{2,1,0:T(8,128)(2,1)S(1)} %gather_fusion.1, pred[8]{0:T(512)(128)(4,1)S(1)} %get-tuple-element.5), kind=kLoop, calls=%fused_computation.2 | loop fusion | flops 688128 | bytes 2752520 | tf_op jit(solution)/shard_map/jit(_take)/select_n | solution.py:26
  34.0 0.0 copy-start.1
  34.0 0.0 copy-start.2
  34.0 5.6 %all-to-all-start = ((bf16[8,112,768]{2,1,0:T(8,128)(2,1)}), bf16[8,112,768]{2,1,0:T(8,128)(2,1)S(1)}, u32[]{:S(2)}, u32[]{:S(2)}) async-start(bf16[8,112,768]{2,1,0:T(8,128)(2,1)} %broadcast_select_fusion), calls=%async_computation | async-start | bytes 2752512 | tf_op jit(solution)/shard_map/all_to_all | solution.py:27
  39.6 0.0 copy-done.1
  39.6 0.6 dynamic_slice.6
  40.9 0.0 copy-done.2
  41.0 1.3 %constant_dynamic-slice_fusion = bf16[896,192]{1,0:T(8,128)(2,1)S(1)} fusion(bf16[896,768]{1,0:T(8,128)(2,1)} %all-gather.2.cloned.1.call-done, s32[]{:T(128)S(6)} %select_n.37), kind=kLoop, calls=%fused_computation.15 | loop fusion | bytes 688132 | tf_op jit(solution)/shard_map/dynamic_slice | solution.py:23
  42.3 0.2 copy.8
  42.5 0.6 gather_fusion
  43.2 29.7 %all-to-all-done = bf16[8,112,768]{2,1,0:T(8,128)(2,1)S(1)} async-done(((bf16[8,112,768]{2,1,0:T(8,128)(2,1)}), bf16[8,112,768]{2,1,0:T(8,128)(2,1)S(1)}, u32[]{:S(2)}, u32[]{:S(2)}) %all-to-all-start) | async-done | bytes 1376288 | tf_op jit(solution)/shard_map/all_to_all | solution.py:27
  72.8 0.6 convolution_bitcast_fusion
  73.4 1.4 %copy.9 = f32[192,1,768]{2,1,0:T(1,128)} copy(f32[192,1,768]{2,0,1:T(8,128)S(1)} %convolution_bitcast_fusion) | data formatting | bytes 1179648 | tf_op jit(solution)/shard_map/reshape | solution.py:30
  (4 shorter events, 0.0 us)
Async XLA Ops:
  6.5 23.6 %copy-start = (bf16[2,112,1,896]{3,1,2,0:T(8,128)(2,1)S(1)}, bf16[2,112,1,896]{3,1,2,0:T(8,128)(2,1)}, u32[]{:S(2)}) copy-start(bf16[2,112,1,896]{3,1,2,0:T(8,128)(2,1)} %param.4) | copy-start | bytes 1204228
  6.5 23.6 %all-gather.2.cloned.1.call-start = ((), (), s32[]{:S(2)}) async-start(), calls=%async_computation.1 | async-start | bytes 1720320 | tf_op jit(solution)/shard_map/all_gather | solution.py:15
  34.0 5.7 %copy-start.1 = (s32[8]{0:T(128)S(1)}, s32[8]{0:T(128)}, u32[]{:S(2)}) copy-start(s32[8]{0:T(128)} %param.7) | copy-start | bytes 100
  34.0 6.9 %copy-start.2 = (s32[8]{0:T(128)S(1)}, s32[8]{0:T(128)}, u32[]{:S(2)}) copy-start(s32[8]{0:T(128)} %param.6) | copy-start | bytes 100
  34.0 38.8 %all-to-all-start = ((bf16[8,112,768]{2,1,0:T(8,128)(2,1)}), bf16[8,112,768]{2,1,0:T(8,128)(2,1)S(1)}, u32[]{:S(2)}, u32[]{:S(2)}) async-start(bf16[8,112,768]{2,1,0:T(8,128)(2,1)} %broadcast_select_fusion), calls=%async_computation | async-start | bytes 2752512 | tf_op jit(solution)/shard_map/all_to_all | solution.py:27
Sparse Core Ops, SparseCore 0:
  8.9 21.2 all-gather.1
where the time goes:
time: 82 us; the launch traced here: 81.7 us
  waiting for transfers between devices  52.6 us (64%)
  between operations  14.1 us (17%)
  starting transfers between devices  5.65 us (7%)
  local copies, waits for them, and re-layouts  4.83 us (6%)
  matrix products  2.45 us (3%)
  other arithmetic  1.99 us (2%)
    all_to_all x1, waiting for transfers between devices, shards(): lax.all_to_all(outgoing, 'pair', split_axis=0, concat_axis=0, tiled=True)  29.7 us
    all_gather x1, waiting for transfers between devices, shards(): all_coeffs = lax.all_gather(coeffs, 'occ', axis=0, tiled=True)  22.2 us
    all_to_all x1, starting transfers between devices, shards(): lax.all_to_all(outgoing, 'pair', split_axis=0, concat_axis=0, tiled=True)  5.65 us
    dot_general x1, matrix products, shards(): jnp.dot(flat_ints, all_coeffs, preferred_element_type=jnp.float32)  1.86 us
  transfers between devices with their start and end apart: 2, of which 2 were waited for; matrix products, arithmetic and copies ran while one was open for 4% of the time, Pallas kernels for 0%

commit v1 on v0

--- a/solution.py
+++ b/solution.py
@@ -1,10 +1,14 @@
+import functools
+
 import jax
 import jax.numpy as jnp
 from jax import lax
+from jax.experimental import pallas as pl
+from jax.experimental.pallas import tpu as pltpu
 from jax.sharding import PartitionSpec as P
 
 
-def shards(half_ints, coeffs, pair_map, tile_table):
+def shards_general(half_ints, coeffs, pair_map, tile_table):
     num_occ = half_ints.shape[0]
     sblock = half_ints.shape[1]
     local_j = half_ints.shape[2]
@@ -30,6 +34,173 @@
     return result.reshape(tile_rows, local_j, num_virt)
 
 
+LANES = 128
+
+
+def kernel(
+    num_pair, num_i, local_tiles,
+    pm_ref, tt_ref, h_ref, c_ref, o_ref,
+    hs, hr, c_all, ct, tiles, ts, tr,
+    c_send, c_recv, f_send, f_recv, p_send, p_recv, h_send, h_recv, t_send, t_recv,
+):
+    me = lax.axis_index("pair")
+    occ = lax.axis_index("occ")
+    sblock, num_virt = c_ref.shape[1], c_ref.shape[2]
+    per = c_ref.shape[0]
+    tile_rows = num_virt // local_tiles
+    half = num_virt // 2
+    partner = occ + 1 - 2 * lax.rem(occ, 2)
+    cross = lax.rem(occ + 2, 4)
+    diagonal = cross + 1 - 2 * lax.rem(cross, 2)
+    peers = [{"pair": lax.rem(me + d, num_pair)} for d in range(1, num_pair)]
+    peers += [{"occ": partner}, {"occ": cross}]
+    barrier = pltpu.get_barrier_semaphore()
+    for peer in peers:
+        pl.semaphore_signal(barrier, inc=1, device_id=peer, device_id_type=pl.DeviceIdType.MESH)
+
+    def remote(source, target, send, recv, where):
+        return pltpu.make_async_remote_copy(
+            src_ref=source, dst_ref=target, send_sem=send, recv_sem=recv,
+            device_id=where, device_id_type=pl.DeviceIdType.MESH,
+        )
+
+    pad = jnp.zeros((sblock, LANES - sblock), jnp.bfloat16)
+    for p in range(num_pair):
+        for i in range(num_i):
+            piece = h_ref[i, :, p * sblock:(p + 1) * sblock]
+            hs[p, :, i * LANES:(i + 1) * LANES] = jnp.concatenate([piece, pad], axis=1)
+
+    pl.semaphore_wait(barrier, len(peers))
+
+    chunks = [(h, b) for h in range(2) for b in range(per)]
+    to_cross, relay, from_relay = [], [], []
+    for q, (h, b) in enumerate(chunks):
+        cols = pl.ds(h * half, half)
+        to_cross.append(remote(
+            c_ref.at[b, :, cols], c_all.at[per * occ + b, :, cols],
+            c_send.at[q], c_recv.at[q], {"occ": cross}))
+        spot = c_all.at[per * cross + b, :, cols]
+        relay.append(remote(spot, spot, f_send.at[q], f_recv.at[q], {"occ": partner}))
+    to_partner = remote(
+        c_ref, c_all.at[pl.ds(per * occ, per)], p_send, p_recv, {"occ": partner})
+    for copy in to_cross:
+        copy.start()
+    to_partner.start()
+    h_copies = []
+    for d in range(1, num_pair):
+        dest = lax.rem(me + d, num_pair)
+        h_copies.append(remote(
+            hs.at[dest], hr.at[d], h_send.at[d], h_recv.at[d], {"pair": dest}))
+    for copy in h_copies:
+        copy.start()
+
+    def turn(owner, b, h):
+        block = c_all[per * owner + b, :, h * half:(h + 1) * half]
+        ct[per * owner + b, h * half:(h + 1) * half, :] = block.T
+
+    for b in range(per):
+        c_all[per * occ + b] = c_ref[b]
+    for h, b in chunks:
+        turn(occ, b, h)
+    to_partner.wait_recv()
+    for h, b in chunks:
+        turn(partner, b, h)
+    for q, (h, b) in enumerate(chunks):
+        to_cross[q].wait_recv()
+        relay[q].start()
+        turn(cross, b, h)
+    for q, (h, b) in enumerate(chunks):
+        relay[q].wait_recv()
+        turn(diagonal, b, h)
+    for copy in h_copies:
+        copy.wait_recv()
+
+    for j in range(local_tiles):
+        rows = slice(j * tile_rows, (j + 1) * tile_rows)
+        total = jnp.zeros((tile_rows, num_i * LANES), jnp.float32)
+        for d in range(num_pair):
+            src = lax.rem(me + num_pair - d, num_pair)
+            block = hs[me] if d == 0 else hr[d]
+            total += jnp.dot(ct[pm_ref[src], rows, :], block, preferred_element_type=jnp.float32)
+        total = total.astype(jnp.bfloat16)
+        for i in range(num_i):
+            tiles[i * local_tiles + j] = total[:, i * LANES:i * LANES + sblock]
+
+    t_copies = []
+    for d in range(1, num_pair):
+        dest = lax.rem(me + d, num_pair)
+        ts[d] = tiles[tt_ref[dest]]
+        copy = remote(ts.at[d], tr.at[d], t_send.at[d], t_recv.at[d], {"pair": dest})
+        copy.start()
+        t_copies.append(copy)
+    tr[0] = tiles[tt_ref[me]]
+    for copy in t_copies:
+        copy.wait_recv()
+    wide = 2 * LANES
+    per_row = num_virt // LANES
+    for n in range(num_virt // wide):
+        total = jnp.zeros((tile_rows, wide), jnp.float32)
+        for d in range(num_pair):
+            src = lax.rem(me + num_pair - d, num_pair)
+            total += jnp.dot(
+                tr[d], c_all[src, :, n * wide:(n + 1) * wide], preferred_element_type=jnp.float32)
+        for m in range(2):
+            o_ref[pl.ds(2 * n + m, tile_rows, stride=per_row), :] = total[:, m * LANES:(m + 1) * LANES]
+
+    for copy in to_cross + relay + [to_partner] + h_copies + t_copies:
+        copy.wait_send()
+
+
+def shards_kernel(half_ints, coeffs, pair_map, tile_table):
+    num_i, sblock, local_j, num_basis = half_ints.shape
+    num_virt = coeffs.shape[1]
+    num_pair = lax.axis_size("pair")
+    local_tiles = num_pair // num_i
+    tile_rows = num_virt // local_tiles
+    per = coeffs.shape[0] // sblock
+    ints = half_ints.reshape(num_i, sblock, num_basis)
+    mine = coeffs.reshape(per, sblock, num_virt)
+    bf16 = jnp.bfloat16
+    dma = pltpu.SemaphoreType.DMA
+    vmem = pl.BlockSpec(memory_space=pltpu.VMEM)
+    smem = pl.BlockSpec(memory_space=pltpu.SMEM)
+    out = pl.pallas_call(
+        functools.partial(kernel, num_pair, num_i, local_tiles),
+        out_shape=jax.ShapeDtypeStruct((tile_rows * num_virt // LANES, LANES), jnp.float32),
+        in_specs=[smem, smem, vmem, vmem],
+        out_specs=vmem,
+        scratch_shapes=[
+            pltpu.VMEM((num_pair, sblock, num_i * LANES), bf16),
+            pltpu.VMEM((num_pair, sblock, num_i * LANES), bf16),
+            pltpu.VMEM((num_pair, sblock, num_virt), bf16),
+            pltpu.VMEM((num_pair, num_virt, sblock), bf16),
+            pltpu.VMEM((num_pair, tile_rows, sblock), bf16),
+            pltpu.VMEM((num_pair, tile_rows, sblock), bf16),
+            pltpu.VMEM((num_pair, tile_rows, sblock), bf16),
+            dma((2 * per,)), dma((2 * per,)), dma((2 * per,)), dma((2 * per,)),
+            dma, dma,
+            dma((num_pair,)), dma((num_pair,)), dma((num_pair,)), dma((num_pair,)),
+        ],
+        compiler_params=pltpu.CompilerParams(
+            collective_id=0, has_side_effects=True, vmem_limit_bytes=40 * 1024 * 1024),
+    )(pair_map, tile_table, ints, mine)
+    return out.reshape(tile_rows, local_j, num_virt)
+
+
+def shards(half_ints, coeffs, pair_map, tile_table):
+    num_i, sblock, local_j, num_basis = half_ints.shape
+    num_virt = coeffs.shape[1]
+    num_pair = lax.axis_size("pair")
+    fits = (
+        num_i == 2 and local_j == 1 and lax.axis_size("occ") == 4
+        and sblock % 16 == 0 and sblock < LANES and sblock * num_pair == num_basis
+        and num_pair % 4 == 0 and num_virt % (2 * LANES) == 0
+        and num_virt % (16 * (num_pair // num_i)) == 0
+    )
+    body = shards_kernel if fits else shards_general
+    return body(half_ints, coeffs, pair_map, tile_table)
+
+
 def solution(mesh):
     placed = (P(None, "pair", "occ", None), P("occ", None), P(), P())
     return jax.shard_map(

time: 82 us -> 31.3 us (0.38)
  the two profiles are of different devices: /device:TPU:0 before, /device:TPU:26 now
where the time goes in v1:
time: 31.3 us; the launch traced here: 31.1 us
  Pallas kernels  27.6 us (88%)
  local copies, waits for them, and re-layouts  3.46 us (11%)
    pallas_call x1, Pallas kernels, shards_kernel(): pl.pallas_call(functools.partial(kernel, num_pair, num_i, local_tiles), o...  27.6 us
    unnamed x9, local copies, waits for them, and re-layouts  3.46 us

profile of v1, /device:TPU:26, one launch (start us, length us, event | category | flops | bytes accessed | tf_op | source)
XLA Modules:
  0.0 31.1 jit_solution(11467089776673408959)
XLA Ops:
  0.0 0.0 copy-start.2
  0.0 0.0 copy-start.3
  0.0 0.7 %copy-done.2 = s32[8]{0:T(128)S(1)} copy-done((s32[8]{0:T(128)S(1)}, s32[8]{0:T(128)}, u32[]{:S(2)}) %copy-start.2) | copy-done | bytes 56
  0.7 0.0 copy-done.3
  0.7 0.0 copy-start
  0.7 1.0 %copy-done = bf16[2,112,1,896]{3,1,2,0:T(8,128)(2,1)S(1)} copy-done((bf16[2,112,1,896]{3,1,2,0:T(8,128)(2,1)S(1)}, bf16[2,112,1,896]{3,1,2,0:T(8,128)(2,1)}, u32[]{:S(2)}) %copy-start) | copy-done | bytes 401432
  1.7 0.0 copy-start.1
  1.7 1.0 %copy-done.1 = bf16[224,768]{1,0:T(8,128)(2,1)S(1)} copy-done((bf16[224,768]{1,0:T(8,128)(2,1)S(1)}, bf16[224,768]{1,0:T(8,128)(2,1)}, u32[]{:S(2)}) %copy-start.1) | copy-done | bytes 344088
  2.6 27.6 %shard_map.46 = f32[1152,128]{1,0:T(8,128)S(1)} custom-call(s32[8]{0:T(128)S(1)} %copy-done.2, s32[8]{0:T(128)S(1)} %copy-done.3, bf16[2,112,896]{2,1,0:T(8,128)(2,1)S(1)} %bitcast.4, bf16[2,112,768]{2,1,0:T(8,128)(2,1)S(1)} %bitcast.5), custom_call_target="tpu_custom_call" | custom-call | tf_op jit(solution)/shard_map/pallas_call | solution.py:167
  30.3 0.8 %copy.7 = f32[192,1,768]{2,1,0:T(1,128)} copy(f32[192,1,768]{2,1,0:T(1,128)S(1)} %bitcast.3) | data formatting | bytes 1179648
Async XLA Ops:
  0.0 0.7 %copy-start.2 = (s32[8]{0:T(128)S(1)}, s32[8]{0:T(128)}, u32[]{:S(2)}) copy-start(s32[8]{0:T(128)} %pm_ref.1) | copy-start | bytes 100
  0.0 0.7 %copy-start.3 = (s32[8]{0:T(128)S(1)}, s32[8]{0:T(128)}, u32[]{:S(2)}) copy-start(s32[8]{0:T(128)} %tt_ref.1) | copy-start | bytes 100
  0.7 1.0 %copy-start = (bf16[2,112,1,896]{3,1,2,0:T(8,128)(2,1)S(1)}, bf16[2,112,1,896]{3,1,2,0:T(8,128)(2,1)}, u32[]{:S(2)}) copy-start(bf16[2,112,1,896]{3,1,2,0:T(8,128)(2,1)} %param.4) | copy-start | bytes 1204228
  1.7 1.0 %copy-start.1 = (bf16[224,768]{1,0:T(8,128)(2,1)S(1)}, bf16[224,768]{1,0:T(8,128)(2,1)}, u32[]{:S(2)}) copy-start(bf16[224,768]{1,0:T(8,128)(2,1)} %param.5) | copy-start | bytes 1032196

commit v2 on v1

v2 whole, which is shorter than its diff:
```python
import functools

import jax
import jax.numpy as jnp
from jax import lax
from jax.experimental import pallas as pl
from jax.experimental.pallas import tpu as pltpu
from jax.sharding import PartitionSpec as P


def shards_general(half_ints, coeffs, pair_map, tile_table):
    num_occ = half_ints.shape[0]
    sblock = half_ints.shape[1]
    local_j = half_ints.shape[2]
    num_basis = half_ints.shape[3]
    num_virt = coeffs.shape[1]
    num_pair = lax.axis_size("pair")
    tile_rows = num_occ * num_virt // num_pair
    all_coeffs = lax.all_gather(coeffs, "occ", axis=0, tiled=True)
    flat_ints = half_ints.reshape(num_occ * sblock * local_j, num_basis)
    half_mo = jnp.dot(flat_ints, all_coeffs, preferred_element_type=jnp.float32).astype(
        jnp.bfloat16
    )
    half_mo = half_mo.reshape(num_occ, sblock, local_j, num_virt)
    tile_id = tile_table[lax.axis_index("pair")]
    virt_start = tile_id * tile_rows % num_virt
    column_coeffs = lax.dynamic_slice_in_dim(all_coeffs, virt_start, tile_rows, 1)
    half_flat = half_mo.reshape(num_occ, sblock, local_j * num_virt)
    slot_occ = tile_table * tile_rows // num_virt
    outgoing = jnp.take(half_flat, slot_occ, axis=0)
    incoming = lax.all_to_all(outgoing, "pair", split_axis=0, concat_axis=0, tiled=True)
    block_coeffs = jnp.take(column_coeffs.reshape(num_pair, sblock, tile_rows), pair_map, axis=0)
    result = jnp.einsum("psa,psc->ac", block_coeffs, incoming, preferred_element_type=jnp.float32)
    return result.reshape(tile_rows, local_j, num_virt)


LANES = 128


def kernel(
    num_pair, num_i, local_tiles,
    pm_hbm, tt_hbm, h_hbm, c_ref, o_ref,
    pm_ref, tt_ref, h_ref, in_sem, hs, hr, c_all, ct, half_sum, tiles, ts, tr, out_sum,
    c_send, c_recv, f_send, f_recv, p_send, p_recv, h_send, h_recv, t_send, t_recv, ring_sem, side_sem,
):
    me = lax.axis_index("pair")
    occ = lax.axis_index("occ")
    ring = num_pair // 2
    z, y = me // 2, lax.rem(me, 2)
    sblock, num_virt = c_ref.shape[1], c_ref.shape[2]
    per = c_ref.shape[0]
    tile_rows = num_virt // local_tiles
    half = num_virt // 2
    partner = occ + 1 - 2 * lax.rem(occ, 2)
    cross = lax.rem(occ + 2, 4)
    diagonal = cross + 1 - 2 * lax.rem(cross, 2)
    MESH = pl.DeviceIdType.MESH

    def ahead(k):
        return 2 * lax.rem(z + k // 2, ring) + lax.rem(y + k, 2)

    def behind(k):
        return 2 * lax.rem(z + ring - k // 2, ring) + lax.rem(y + k, 2)

    near = (1, 2, 2 * ring - 2)
    groups = ((0, 1, 2, 6), (3, 7, 4), (5,))
    send_order = (5, 4, 3, 7, 2, 6, 1)

    fetch_c = pltpu.make_async_copy(c_ref, c_all.at[pl.ds(per * occ, per)], in_sem.at[1])
    fetch_h = pltpu.make_async_copy(h_hbm, h_ref, in_sem.at[0])
    fetch_pm = pltpu.make_async_copy(pm_hbm, pm_ref, in_sem.at[2])
    fetch_tt = pltpu.make_async_copy(tt_hbm, tt_ref, in_sem.at[3])
    barrier = pltpu.get_barrier_semaphore()
    greeted = [{"occ": partner}, {"occ": cross}] + [{"pair": ahead(k)} for k in range(1, num_pair)]
    for peer in greeted:
        pl.semaphore_signal(barrier, inc=1, device_id=peer, device_id_type=MESH)
    for fetch in (fetch_h, fetch_c, fetch_pm, fetch_tt):
        fetch.start()

    def remote(source, target, send, recv, where):
        return pltpu.make_async_remote_copy(
            src_ref=source, dst_ref=target, send_sem=send, recv_sem=recv,
            device_id=where, device_id_type=MESH,
        )

    chunks = [(h, b) for h in range(2) for b in range(per)]
    to_cross, relay = [], []
    for q, (h, b) in enumerate(chunks):
        cols = pl.ds(h * half, half)
        to_cross.append(remote(
            c_ref.at[b, :, cols], c_all.at[per * occ + b, :, cols],
            c_send.at[q], c_recv.at[q], {"occ": cross}))
        spot = c_all.at[per * cross + b, :, cols]
        relay.append(remote(spot, spot, f_send.at[q], f_recv.at[q], {"occ": partner}))
    to_partner = remote(
        c_ref, c_all.at[pl.ds(per * occ, per)], p_send, p_recv, {"occ": partner})
    h_copies = {
        k: remote(hs.at[ahead(k)], hr.at[k], h_send.at[k], h_recv.at[k], {"pair": ahead(k)})
        for k in range(1, num_pair)}
    t_copies = {
        k: remote(ts.at[k], tr.at[k], t_send.at[k], t_recv.at[k], {"pair": ahead(k)})
        for k in range(1, num_pair)}

    fetch_h.wait()
    pad = jnp.zeros((sblock, LANES - sblock), jnp.bfloat16)
    for p in range(num_pair):
        for i in range(num_i):
            piece = h_ref[i, :, p * sblock:(p + 1) * sblock]
            hs[p, :, i * LANES:(i + 1) * LANES] = jnp.concatenate([piece, pad], axis=1)

    pl.semaphore_wait(barrier, len(greeted))
    for copy in to_cross:
        copy.start()
    to_partner.start()

    early = ()
    for k in early:
        h_copies[k].start()
    for n in range(1, num_pair):
        k = (0, 1, 2, 3, 4, 5, 6, 7)[n] + y * ((0, 3, 2, 5, 4, 7, 6, 1)[n] - (0, 1, 2, 3, 4, 5, 6, 7)[n])
        remote(hs.at[ahead(k)], hr.at[k], h_send.at[k], h_recv.at[k], {"pair": ahead(k)}).start()

    def turn(owner, b, h):
        block = c_all[per * owner + b, :, h * half:(h + 1) * half]
        ct[per * owner + b, h * half:(h + 1) * half, :] = block.T

    for fetch in (fetch_c, fetch_pm, fetch_tt):
        fetch.wait()
    for h, b in chunks:
        turn(occ, b, h)
    to_partner.wait_recv()
    for h, b in chunks:
        turn(partner, b, h)
    for q, (h, b) in enumerate(chunks):
        to_cross[q].wait_recv()
        relay[q].start()
        turn(cross, b, h)
    for q, (h, b) in enumerate(chunks):
        relay[q].wait_recv()
        turn(diagonal, b, h)

    last = len(groups) - 1
    for g, group in enumerate(groups):
        for k in group:
            if k > 0:
                h_copies[k].wait_recv()
        for j in range(local_tiles):
            rows = slice(j * tile_rows, (j + 1) * tile_rows)
            total = half_sum[rows, :] if g > 0 else None
            for k in group:
                block = hs[me] if k == 0 else hr[k]
                term = jnp.dot(
                    ct[pm_ref[behind(k)], rows, :], block, preferred_element_type=jnp.float32)
                total = term if total is None else total + term
            if g < last:
                half_sum[rows, :] = total
            else:
                total = total.astype(jnp.bfloat16)
                for i in range(num_i):
                    tiles[i * local_tiles + j] = total[:, i * LANES:i * LANES + sblock]

    for n in range(1, num_pair):
        k = (0, 1, 2, 3, 4, 5, 6, 7)[n] + y * ((0, 3, 2, 5, 4, 7, 6, 1)[n] - (0, 1, 2, 3, 4, 5, 6, 7)[n])
        ts[k] = tiles[tt_ref[ahead(k)]]
        remote(ts.at[k], tr.at[k], t_send.at[k], t_recv.at[k], {"pair": ahead(k)}).start()
    tr[0] = tiles[tt_ref[me]]
    wide = 2 * LANES
    per_row = num_virt // LANES
    for g, group in enumerate(groups):
        for k in group:
            if k > 0:
                t_copies[k].wait_recv()
        for n in range(num_virt // wide):
            cols = slice(n * wide, (n + 1) * wide)
            total = out_sum[:, cols] if g > 0 else None
            for k in group:
                term = jnp.dot(
                    tr[k], c_all[behind(k), :, cols], preferred_element_type=jnp.float32)
                total = term if total is None else total + term
            if g < last:
                out_sum[:, cols] = total
            else:
                for m in range(2):
                    o_ref[pl.ds(2 * n + m, tile_rows, stride=per_row), :] = (
                        total[:, m * LANES:(m + 1) * LANES])

    for copy in to_cross + relay + [to_partner] + list(h_copies.values()) + list(t_copies.values()):
        copy.wait_send()


def shards_kernel(half_ints, coeffs, pair_map, tile_table):
    num_i, sblock, local_j, num_basis = half_ints.shape
    num_virt = coeffs.shape[1]
    num_pair = lax.axis_size("pair")
    local_tiles = num_pair // num_i
    tile_rows = num_virt // local_tiles
    per = coeffs.shape[0] // sblock
    ints = half_ints.reshape(num_i, sblock, num_basis)
    mine = coeffs.reshape(per, sblock, num_virt)
    bf16 = jnp.bfloat16
    dma = pltpu.SemaphoreType.DMA
    vmem = pl.BlockSpec(memory_space=pltpu.VMEM)
    hbm = pl.BlockSpec(memory_space=pltpu.HBM)
    ints, mine, pair_map, tile_table = (
        pltpu.with_memory_space_constraint(a, pltpu.HBM) for a in (ints, mine, pair_map, tile_table))
    out = pl.pallas_call(
        functools.partial(kernel, num_pair, num_i, local_tiles),
        out_shape=jax.ShapeDtypeStruct((tile_rows * num_virt // LANES, LANES), jnp.float32),
        in_specs=[hbm, hbm, hbm, hbm],
        out_specs=vmem,
        scratch_shapes=[
            pltpu.SMEM(pair_map.shape, jnp.int32),
            pltpu.SMEM(tile_table.shape, jnp.int32),
            pltpu.VMEM(ints.shape, bf16),
            dma((4,)),
            pltpu.VMEM((num_pair, sblock, num_i * LANES), bf16),
            pltpu.VMEM((num_pair, sblock, num_i * LANES), bf16),
            pltpu.VMEM((num_pair, sblock, num_virt), bf16),
            pltpu.VMEM((num_pair, num_virt, sblock), bf16),
            pltpu.VMEM((num_virt, num_i * LANES), jnp.float32),
            pltpu.VMEM((num_pair, tile_rows, sblock), bf16),
            pltpu.VMEM((num_pair, tile_rows, sblock), bf16),
            pltpu.VMEM((num_pair, tile_rows, sblock), bf16),
            pltpu.VMEM((tile_rows, num_virt), jnp.float32),
            dma((2 * per,)), dma((2 * per,)), dma((2 * per,)), dma((2 * per,)),
            dma, dma,
            dma((num_pair,)), dma((num_pair,)), dma((num_pair,)), dma((num_pair,)),
            pltpu.SemaphoreType.REGULAR, pltpu.SemaphoreType.REGULAR,
        ],
        compiler_params=pltpu.CompilerParams(
            collective_id=0, has_side_effects=True, vmem_limit_bytes=40 * 1024 * 1024),
    )(pair_map, tile_table, ints, mine)
    return out.reshape(tile_rows, local_j, num_virt)


def shards(half_ints, coeffs, pair_map, tile_table):
    num_i, sblock, local_j, num_basis = half_ints.shape
    num_virt = coeffs.shape[1]
    num_pair = lax.axis_size("pair")
    fits = (
        num_i == 2 and local_j == 1 and lax.axis_size("occ") == 4
        and sblock % 16 == 0 and sblock < LANES and sblock * num_pair == num_basis
        and num_pair == 8 and num_virt % (2 * LANES) == 0
        and num_virt % (16 * (num_pair // num_i)) == 0
    )
    body = shards_kernel if fits else shards_general
    return body(half_ints, coeffs, pair_map, tile_table)


def solution(mesh):
    placed = (P(None, "pair", "occ", None), P("occ", None), P(), P())
    return jax.shard_map(
        shards, mesh=mesh, in_specs=placed, out_specs=P("pair", "occ", None), check_vma=False
    )
```

time: 31.3 us -> 27.3 us (0.87)
  the two profiles are of different devices: /device:TPU:26 before, /device:TPU:13 now
where the time goes in v2:
time: 27.3 us; the launch traced here: 27.2 us
  Pallas kernels  26.3 us (96%)
  local copies, waits for them, and re-layouts  0.82 us (3%)
    pallas_call x1, Pallas kernels, shards_kernel(): pl.pallas_call(functools.partial(kernel, num_pair, num_i, local_tiles), o...  26.3 us
    unnamed x1, local copies, waits for them, and re-layouts  0.82 us

profile of v2, /device:TPU:13, one launch (start us, length us, event | category | flops | bytes accessed | tf_op | source)
XLA Modules:
  0.0 27.2 jit_solution(11264934801216886404)
XLA Ops:
  0.0 26.3 %shard_map.46 = f32[1152,128]{1,0:T(8,128)S(1)} custom-call(s32[8]{0:T(128)} %pm_hbm.1, s32[8]{0:T(128)} %tt_hbm.1, bf16[2,112,896]{2,1,0:T(8,128)(2,1)} %bitcast.4, bf16[2,112,768]{2,1,0:T(8,128)(2,1)} %bitcast.5), custom_call_target="tpu_custom_call" | custom-call | tf_op jit(solution)/shard_map/pallas_call | solution.py:206
  26.4 0.8 %copy.7 = f32[192,1,768]{2,1,0:T(1,128)} copy(f32[192,1,768]{2,1,0:T(1,128)S(1)} %bitcast.3) | data formatting | bytes 1179648

commit v3 on v2

--- a/solution.py
+++ b/solution.py
@@ -41,7 +41,7 @@
     num_pair, num_i, local_tiles,
     pm_hbm, tt_hbm, h_hbm, c_ref, o_ref,
     pm_ref, tt_ref, h_ref, in_sem, hs, hr, c_all, ct, half_sum, tiles, ts, tr, out_sum,
-    c_send, c_recv, f_send, f_recv, p_send, p_recv, h_send, h_recv, t_send, t_recv, ring_sem, side_sem,
+    c_send, c_recv, f_send, f_recv, p_send, p_recv, h_send, h_recv, t_send, t_recv,
 ):
     me = lax.axis_index("pair")
     occ = lax.axis_index("occ")
@@ -50,7 +50,7 @@
     sblock, num_virt = c_ref.shape[1], c_ref.shape[2]
     per = c_ref.shape[0]
     tile_rows = num_virt // local_tiles
-    half = num_virt // 2
+    half = num_virt
     partner = occ + 1 - 2 * lax.rem(occ, 2)
     cross = lax.rem(occ + 2, 4)
     diagonal = cross + 1 - 2 * lax.rem(cross, 2)
@@ -62,9 +62,7 @@
     def behind(k):
         return 2 * lax.rem(z + ring - k // 2, ring) + lax.rem(y + k, 2)
 
-    near = (1, 2, 2 * ring - 2)
     groups = ((0, 1, 2, 6), (3, 7, 4), (5,))
-    send_order = (5, 4, 3, 7, 2, 6, 1)
 
     fetch_c = pltpu.make_async_copy(c_ref, c_all.at[pl.ds(per * occ, per)], in_sem.at[1])
     fetch_h = pltpu.make_async_copy(h_hbm, h_ref, in_sem.at[0])
@@ -83,17 +81,17 @@
             device_id=where, device_id_type=MESH,
         )
 
-    chunks = [(h, b) for h in range(2) for b in range(per)]
+    chunks = [(h, b) for h in range(1) for b in range(per)]
     to_cross, relay = [], []
     for q, (h, b) in enumerate(chunks):
         cols = pl.ds(h * half, half)
         to_cross.append(remote(
-            c_ref.at[b, :, cols], c_all.at[per * occ + b, :, cols],
+            c_all.at[per * occ + b, :, cols], c_all.at[per * occ + b, :, cols],
             c_send.at[q], c_recv.at[q], {"occ": cross}))
         spot = c_all.at[per * cross + b, :, cols]
         relay.append(remote(spot, spot, f_send.at[q], f_recv.at[q], {"occ": partner}))
     to_partner = remote(
-        c_ref, c_all.at[pl.ds(per * occ, per)], p_send, p_recv, {"occ": partner})
+        c_all.at[pl.ds(per * occ, per)], c_all.at[pl.ds(per * occ, per)], p_send, p_recv, {"occ": partner})
     h_copies = {
         k: remote(hs.at[ahead(k)], hr.at[k], h_send.at[k], h_recv.at[k], {"pair": ahead(k)})
         for k in range(1, num_pair)}
@@ -108,14 +106,13 @@
             piece = h_ref[i, :, p * sblock:(p + 1) * sblock]
             hs[p, :, i * LANES:(i + 1) * LANES] = jnp.concatenate([piece, pad], axis=1)
 
+    fetch_c.wait()
     pl.semaphore_wait(barrier, len(greeted))
     for copy in to_cross:
         copy.start()
     to_partner.start()
 
-    early = ()
-    for k in early:
-        h_copies[k].start()
+
     for n in range(1, num_pair):
         k = (0, 1, 2, 3, 4, 5, 6, 7)[n] + y * ((0, 3, 2, 5, 4, 7, 6, 1)[n] - (0, 1, 2, 3, 4, 5, 6, 7)[n])
         remote(hs.at[ahead(k)], hr.at[k], h_send.at[k], h_recv.at[k], {"pair": ahead(k)}).start()
@@ -124,7 +121,7 @@
         block = c_all[per * owner + b, :, h * half:(h + 1) * half]
         ct[per * owner + b, h * half:(h + 1) * half, :] = block.T
 
-    for fetch in (fetch_c, fetch_pm, fetch_tt):
+    for fetch in (fetch_pm, fetch_tt):
         fetch.wait()
     for h, b in chunks:
         turn(occ, b, h)
@@ -225,7 +222,6 @@
             dma((2 * per,)), dma((2 * per,)), dma((2 * per,)), dma((2 * per,)),
             dma, dma,
             dma((num_pair,)), dma((num_pair,)), dma((num_pair,)), dma((num_pair,)),
-            pltpu.SemaphoreType.REGULAR, pltpu.SemaphoreType.REGULAR,
         ],
         compiler_params=pltpu.CompilerParams(
             collective_id=0, has_side_effects=True, vmem_limit_bytes=40 * 1024 * 1024),

time: 27.3 us -> 27.1 us (level)
  Pallas kernels: 26.3 us -> 25.9 us
    pallas_call x1, Pallas kernels: 26.3 us -> 25.9 us  [shards_kernel(): pl.pallas_call(functools.partial(kernel, num_pair, num_i, local_tiles), o...]
where the time goes in v3:
time: 27.1 us; the launch traced here: 26.8 us
  Pallas kernels  25.9 us (96%)
  local copies, waits for them, and re-layouts  0.82 us (3%)
    pallas_call x1, Pallas kernels, shards_kernel(): pl.pallas_call(functools.partial(kernel, num_pair, num_i, local_tiles), o...  25.9 us
    unnamed x1, local copies, waits for them, and re-layouts  0.82 us

profile of v3, /device:TPU:13, one launch (start us, length us, event | category | flops | bytes accessed | tf_op | source)
XLA Modules:
  0.0 26.8 jit_solution(1297700081866290109)
XLA Ops:
  0.0 25.9 %shard_map.46 = f32[1152,128]{1,0:T(8,128)S(1)} custom-call(s32[8]{0:T(128)} %pm_hbm.1, s32[8]{0:T(128)} %tt_hbm.1, bf16[2,112,896]{2,1,0:T(8,128)(2,1)} %bitcast.4, bf16[2,112,768]{2,1,0:T(8,128)(2,1)} %bitcast.5), custom_call_target="tpu_custom_call" | custom-call | tf_op jit(solution)/shard_map/pallas_call | solution.py:203
  25.9 0.8 %copy.7 = f32[192,1,768]{2,1,0:T(1,128)} copy(f32[192,1,768]{2,1,0:T(1,128)S(1)} %bitcast.3) | data formatting | bytes 1179648
